TPU v7x, 32 devices: a whole 2x2x4 slice. The times are simulated.
32 devices in a mesh: groups: 2 (over x), ctx: 16 (over z, y, core).
Axes of the slice: x: 2, y: 2, z: 4, core: 2. Of those that a mesh axis runs over, the one named last changes fastest.
Arguments:
- gate_short: bfloat16 [4096, 4096], P(('groups', 'ctx')), parts along dimension 0, may hold values from -6 to 6
- key_short: bfloat16 [4096, 4096], P(('groups', 'ctx')), parts along dimension 0, may hold values from -6 to 6
- value_short: bfloat16 [4096, 4096], P(('groups', 'ctx')), parts along dimension 0, may hold values from -6 to 6
- gate_long: bfloat16 [4096, 4096], P(('groups', 'ctx')), parts along dimension 0, may hold values from -6 to 6
- doc_ids: int32 [4096], P(('groups', 'ctx')), parts along dimension 0, may hold values from 0 to 7, never falling along the last dimension, each value on 1 to 512 neighbouring positions
- se_filter: float32 [7, 256], replicated, may hold values from -2 to 2
- long_filter: bfloat16 [256, 512], replicated, may hold values from -1.25 to 1.25
Outputs:
- scored: bfloat16 [4096, 4096], P(('groups', 'ctx')), parts along dimension 0
There are 2 independent parts, one for each index of `groups`. A program takes and returns all parts, laid end to end along the dimension named above; an argument that names none is the same for every part. Nothing has to cross between parts.
Inputs may be any that keep to these rules, and one draw needn't show every extreme that they name: doc_ids never falls along the rows of a group; each document holds 1 to 512 consecutive rows, and one holds exactly 512.
All inputs are finite; a program needn't handle non-finite values.
Results may differ from a plain program's by a relative error of at most 0.0057.
Values may be sent and summed in bfloat16 or wider, within the bound.
A program may use at most 192 MiB of HBM per device.

v0:
```python
import jax
import jax.numpy as jnp
from jax import lax
from jax.sharding import PartitionSpec as P

STRETCH = 128
MAXDOC = 512
REACH = 4


def passed_along(value, axis, steps):
    count = lax.axis_size(axis)
    first, last = (max(0, -steps), min(count, count - steps))
    return lax.ppermute(value, axis, [(source, source + steps) for source in range(first, last)])


def shortened(value):

    def short(part):
        return part.astype(jnp.bfloat16) if part.dtype == jnp.float32 else part

    return jax.tree.map(short, value)


def short_mixing(key_value, rim_value, doc_ids, rim_doc, se_filter):
    row_count, chan_count = key_value.shape
    tap_count, filter_count = se_filter.shape
    widened = jnp.repeat(se_filter, chan_count // filter_count, axis=1)
    joined = jnp.concatenate([rim_value, key_value], 0)
    joined_doc = jnp.concatenate([rim_doc, doc_ids], 0)
    summed = jnp.zeros((row_count, chan_count), jnp.float32)
    for tap_index in range(tap_count):
        offset = tap_count - 1 - tap_index
        shifted = lax.slice_in_dim(joined, offset, offset + row_count, axis=0).astype(jnp.float32)
        agreeing = (
            lax.slice_in_dim(joined_doc, offset, offset + row_count, axis=0) == doc_ids
        ).astype(jnp.float32)
        summed = summed + widened[tap_index][None, :] * agreeing[:, None] * shifted
    return summed


def tile_product(operands):
    far_taps, gathered = operands
    return jnp.einsum("gtp,gkip->gkit", far_taps, gathered, preferred_element_type=jnp.float32)


def body(gate_short, key_short, value_short, gate_long, doc_ids, se_filter, long_filter):
    row_count, chan_count = gate_short.shape
    tap_count, filter_count = se_filter.shape
    group_width = chan_count // filter_count
    key_value = (key_short.astype(jnp.float32) * value_short.astype(jnp.float32)).astype(
        jnp.bfloat16
    )
    rim_value, rim_doc = passed_along(
        (key_value[row_count - (tap_count - 1) :], doc_ids[row_count - (tap_count - 1) :]), "ctx", 1
    )
    local_value = lax.optimization_barrier(key_value)
    short_mix = short_mixing(local_value, rim_value, doc_ids, rim_doc, se_filter)
    mixed = (gate_short.astype(jnp.float32) * short_mix).astype(jnp.bfloat16)
    mixed_cols = mixed.T
    per_device = row_count // STRETCH
    span_count = MAXDOC // STRETCH
    blocks = [(mixed_cols, doc_ids)]
    stride = 1
    while len(blocks) <= REACH:
        wanted = min(stride, REACH + 1 - len(blocks))
        sent_rows = jnp.stack([entry_pair[0] for entry_pair in blocks[:wanted]])
        sent_docs = jnp.stack([entry_pair[1] for entry_pair in blocks[:wanted]])
        got_rows, got_docs = (
            passed_along(sent_rows, "ctx", stride),
            passed_along(shortened(sent_docs), "ctx", stride).astype(sent_docs.dtype),
        )
        for position in range(wanted):
            blocks.append((got_rows[position], got_docs[position]))
        stride = stride * 2
    ordered = blocks[::-1]
    stack_rows = jnp.concatenate([entry_pair[0] for entry_pair in ordered], 1).reshape(
        filter_count, group_width, -1
    )
    stack_docs = jnp.concatenate([entry_pair[1] for entry_pair in ordered], 0)
    own_first = REACH * per_device
    own_rows = stack_rows[:, :, own_first * STRETCH :].reshape(
        filter_count, group_width, per_device, STRETCH
    )
    own_docs = doc_ids.reshape(per_device, STRETCH)
    leaders = own_docs[:, 0]
    padded_filter = jnp.concatenate(
        [long_filter, jnp.zeros((filter_count, STRETCH), jnp.bfloat16)], 1
    )
    target_pos = lax.broadcasted_iota(jnp.int32, (STRETCH, STRETCH), 0)
    source_pos = lax.broadcasted_iota(jnp.int32, (STRETCH, STRETCH), 1)
    near_lag = target_pos - source_pos
    near_taps = jnp.take(padded_filter, jnp.clip(near_lag, 0, STRETCH - 1), axis=1)
    tile_mask = (near_lag >= 0)[None] & (own_docs[:, :, None] == own_docs[:, None, :])
    masked_taps = jnp.where(tile_mask[None], near_taps[:, None], jnp.zeros((), jnp.bfloat16))
    near_total = jnp.einsum(
        "gits,gkis->gkit", masked_taps, own_rows, preferred_element_type=jnp.float32
    )
    far_width = span_count * STRETCH
    window_tgt = lax.broadcasted_iota(jnp.int32, (STRETCH, far_width), 0)
    window_pos = lax.broadcasted_iota(jnp.int32, (STRETCH, far_width), 1)
    far_lag = window_tgt - window_pos + far_width
    far_taps = jnp.take(padded_filter, far_lag, axis=1)
    matches = []
    lowest = (own_first - span_count) * STRETCH
    source_docs = stack_docs[lowest : lowest + far_width]
    agreeing = source_docs == leaders[0]
    matches.append(agreeing)
    source_rows = stack_rows[:, :, lowest : lowest + far_width]
    sources = [jnp.where(agreeing[None, None, :], source_rows, jnp.zeros_like(source_rows))]
    gathered = jnp.stack(sources, 2)
    far_total = tile_product((far_taps, gathered))
    target_mask = (own_docs == leaders[:, None]).astype(jnp.float32)
    long_sum = (near_total + far_total * target_mask[None, None]).reshape(chan_count, row_count).T
    return (gate_long.astype(jnp.float32) * long_sum).astype(jnp.bfloat16)


def solution(mesh):
    placed = (
        P(("groups", "ctx"), None),
        P(("groups", "ctx"), None),
        P(("groups", "ctx"), None),
        P(("groups", "ctx"), None),
        P(("groups", "ctx")),
        P(),
        P(),
    )
    return jax.shard_map(
        body, mesh=mesh, in_specs=placed, out_specs=P(("groups", "ctx"), None), check_vma=False
    )
```

profile of v0, /device:TPU:0, one launch (start us, length us, event | category | flops | bytes accessed | tf_op | source)
XLA Modules:
  0.0 472.4 jit_solution(6332125714934271169)
XLA Ops:
  0.0 1.7 copy.26
  1.7 0.7 copy.25
  2.4 0.3 multiply_convert_fusion.1
  2.7 0.4 slice.146
  3.1 0.4 copy.27
  3.4 2.4 collective-permute-start.1
  5.9 0.1 slice.113
  5.9 4.5 collective-permute-start
  10.5 0.7 copy.24
  11.2 0.1 broadcast_in_dim.96
  11.3 0.1 broadcast_in_dim.97
  11.4 0.1 broadcast_in_dim.94
  11.5 0.1 broadcast_in_dim.95
  11.6 0.1 broadcast_in_dim.92
  11.7 0.1 broadcast_in_dim.93
  11.8 0.1 broadcast_in_dim.90
  11.9 0.1 broadcast_in_dim.91
  12.0 0.1 broadcast_in_dim.88
  12.1 0.1 broadcast_in_dim.89
  12.2 0.1 broadcast_in_dim.86
  12.3 0.1 broadcast_in_dim.87
  12.4 0.1 broadcast_in_dim.84
  12.5 0.1 broadcast_in_dim.85
  12.6 0.1 pad_add_fusion
  12.7 0.1 compare_convert_fusion.6
  12.8 0.5 copy.28
  13.3 7.6 %multiply_convert_fusion = bf16[128,4096]{0,1:T(8,128)(2,1)S(1)} fusion(bf16[128,4096]{0,1:T(8,128)(2,1)S(1)} %multiply_convert_fusion.1, bf16[128,4096]{0,1:T(8,128)(2,1)S(1)} %copy.24, bf16[6,4096]{0,1:T(8,128)(2,1)S(1)} %copy.28, f32[128]{0:T(128)S(1)} %get-tuple-element.15, f32[4096]{0:T(1024)S(1)} %broadcast_in_dim.97, f32[128]{0:T(128)S(1)} %get-tuple-element.16, ...), kind=kLoop, calls=%fused_computation.38 | loop fusion | flops 24641536 | bytes 3312640 | tf_op jit(solution)/shard_map/convert_element_type | solution.py:59
  20.9 2.0 collective-permute-start.6
  22.9 3.5 collective-permute-start.3
  26.4 3.5 collective-permute-start.2
  29.9 0.1 copy.33
  30.0 1.7 pad_maximum_fusion
  31.7 10.6 %collective-permute-start.7 = (bf16[2,4096,128]{2,1,0:T(8,128)(2,1)}, bf16[2,4096,128]{2,1,0:T(8,128)(2,1)S(1)}, u32[]{:S(2)}, u32[]{:S(2)}) collective-permute-start(bf16[2,4096,128]{2,1,0:T(8,128)(2,1)} %pad_maximum_fusion), channel_id=1, source_target_pairs={{0,2},{1,3},{2,4},{3,5},{4,6},{5,7},{6,8},{7,9},{8,10},{9,11},{10,... | collective-permute-start | bytes 6291464 | tf_op jit(solution)/shard_map/ppermute | solution.py:14
  42.3 0.1 fusion.38
  42.4 4.3 collective-permute-start.4
  46.8 0.1 copy.29
  47.0 65.2 %gather_fusion = bf16[16384,256]{1,0:T(8,128)(2,1)} fusion(bf16[256,640]{0,1:T(8,128)(2,1)S(1)} %concatenate.39, s32[16384]{0:T(1024)S(1)} %fusion.34), kind=kCustom, calls=%fused_computation | custom fusion | bytes 16842752 | tf_op jit(solution)/shard_map/jit(_take)/gather | solution.py:93
  112.1 12.5 %copy.30 = bf16[128,128,256]{1,0,2:T(8,128)(2,1)} copy(bf16[128,128,256]{2,1,0:T(8,128)(2,1)} %bitcast.50) | data formatting | bytes 16777216 | tf_op jit(solution)/shard_map/jit(_take)/gather | solution.py:93
  124.6 257.8 %gather_fusion.1 = bf16[65536,256]{1,0:T(8,128)(2,1)} fusion(bf16[256,640]{0,1:T(8,128)(2,1)S(1)} %concatenate.39, s32[65536]{0:T(1024)S(1)} %broadcast_clamp_fusion), kind=kCustom, calls=%fused_computation.1 | custom fusion | bytes 67371008 | tf_op jit(solution)/shard_map/jit(_take)/gather | solution.py:103
  382.4 44.9 %copy.31 = bf16[128,512,256]{1,0,2:T(8,128)(2,1)} copy(bf16[128,512,256]{2,1,0:T(8,128)(2,1)} %bitcast.49) | data formatting | bytes 67108864 | tf_op jit(solution)/shard_map/jit(_take)/gather | solution.py:103
  427.3 3.6 collective-permute-start.5
  430.9 9.2 %fusion.5 = f32[256,16,128]{2,1,0:T(8,128)} fusion(bf16[256,16,128]{2,1,0:T(8,128)(2,1)S(1)} %bitcast.54, bf16[128,128,256]{1,0,2:T(8,128)(2,1)} %copy.30, pred[128,128]{1,0:T(8,128)(4,1)S(1)} %get-tuple-element.24, pred[128,128]{1,0:T(8,128)(4,1)S(1)} %get-tuple-element.23), kind=kOutput, calls=%fused_computation.7 | convolution fusion | flops 142606336 | bytes 11567104 | tf_op jit(solution)/shard_map/gits,gkis->gkit/dot_general | solution.py:96
  440.1 1.5 fusion.45
  441.5 9.5 %collective-permute-done.5 = bf16[1,4096,128]{2,1,0:T(8,128)(2,1)S(1)} collective-permute-done((bf16[1,4096,128]{2,1,0:T(8,128)(2,1)S(1)}, bf16[1,4096,128]{2,1,0:T(8,128)(2,1)S(1)}, u32[]{:S(2)}, u32[]{:S(2)}) %collective-permute-start.5) | collective-permute-done | bytes 1048608 | tf_op jit(solution)/shard_map/ppermute | solution.py:14
  451.0 1.0 copy-done.9
  452.0 17.1 %multiply_add_fusion = f32[256,16,128]{2,1,0:T(8,128)} fusion(f32[256,16,128]{2,1,0:T(8,128)} %fusion.5, bf16[128,512,256]{1,0,2:T(8,128)(2,1)} %copy.31, pred[128,512]{1,0:T(8,128)(4,1)S(1)} %fusion.32, bf16[256,16,128]{2,1,0:T(8,128)(2,1)} %bitcast.57, bf16[256,16,128]{2,1,0:T(8,128)(2,1)} %bitcast.59, bf16[256,16,128]{2,1,0:T(8,128)(2,1)} %bitcast.58, ...), kind=kOutput, calls=%fused_computation.36 | convolution fusion | flops 573571072 | bytes 42009600 | tf_op jit(solution)/shard_map/gtp,gkip->gkit/dot_general | solution.py:44
  469.1 2.0 copy.32
  471.2 1.2 fusion.20
  (35 shorter events, 0.3 us)
Async XLA Ops:
  0.0 1.7 copy-start.2
  2.7 3.2 copy-start.7
  2.7 7.8 %copy-start.3 = (bf16[128,4096]{1,0:T(8,128)(2,1)S(1)}, bf16[128,4096]{1,0:T(8,128)(2,1)}, u32[]{:S(2)}) copy-start(bf16[128,4096]{1,0:T(8,128)(2,1)} %param.7) | copy-start | bytes 3145732
  3.1 8.1 %copy-start.8 = (f32[7,256]{1,0:T(8,128)S(1)}, f32[7,256]{1,0:T(8,128)}, u32[]{:S(2)}) copy-start(f32[7,256]{1,0:T(8,128)} %param.12) | copy-start | bytes 21508
  3.4 9.4 %collective-permute-start.1 = (bf16[6,4096]{1,0:T(8,128)(2,1)S(1)}, bf16[6,4096]{1,0:T(8,128)(2,1)S(1)}, u32[]{:S(2)}, u32[]{:S(2)}) collective-permute-start(bf16[6,4096]{1,0:T(8,128)(2,1)S(1)} %copy.27), channel_id=1, source_target_pairs={{0,1},{1,2},{2,3},{3,4},{4,5},{5,6},{6,7},{7,8},{8,9},{9,10},{10,1... | collective-permute-start | bytes 147464 | tf_op jit(solution)/shard_map/ppermute | solution.py:14
  5.9 6.7 %collective-permute-start = (s32[6]{0:T(128)S(1)}, s32[6]{0:T(128)S(1)}, u32[]{:S(2)}, u32[]{:S(2)}) collective-permute-start(s32[6]{0:T(128)S(1)} %slice.113), channel_id=1, source_target_pairs={{0,1},{1,2},{2,3},{3,4},{4,5},{5,6},{6,7},{7,8},{8,9},{9,10},{10,1... | collective-permute-start | bytes 80 | tf_op jit(solution)/shard_map/ppermute | solution.py:14
  20.9 10.8 %copy-start = (bf16[128,4096]{0,1:T(8,128)(2,1)}, bf16[128,4096]{0,1:T(8,128)(2,1)S(1)}, u32[]{:S(2)}) copy-start(bf16[128,4096]{0,1:T(8,128)(2,1)S(1)} %multiply_convert_fusion) | copy-start | bytes 3145732
  20.9 9.1 %collective-permute-start.6 = (bf16[1,4096,128]{2,1,0:T(8,128)(2,1)S(1)}, bf16[1,4096,128]{2,1,0:T(8,128)(2,1)S(1)}, u32[]{:S(2)}, u32[]{:S(2)}) collective-permute-start(bf16[1,4096,128]{2,1,0:T(8,128)(2,1)S(1)} %bitcast.51), channel_id=1, source_target_pairs={{0,1},{1,2},{2,3},{3,4},{4,5},{5,6},{6,7},{7,8},{8,9},{9,10},{10,1... | collective-permute-start | bytes 3145736 | tf_op jit(solution)/shard_map/ppermute | solution.py:14
  22.9 19.5 %collective-permute-start.3 = (s32[1,128]{1,0:T(1,128)S(1)}, s32[1,128]{1,0:T(1,128)S(1)}, u32[]{:S(2)}, u32[]{:S(2)}) collective-permute-start(s32[1,128]{1,0:T(1,128)S(1)} %bitcast.61), channel_id=1, source_target_pairs={{0,1},{1,2},{2,3},{3,4},{4,5},{5,6},{6,7},{7,8},{8,9},{9,10},{10,1... | collective-permute-start | bytes 1544 | tf_op jit(solution)/shard_map/ppermute | solution.py:14
  26.4 400.9 %collective-permute-start.2 = (s32[1,128]{1,0:T(1,128)S(1)}, s32[1,128]{1,0:T(1,128)S(1)}, u32[]{:S(2)}, u32[]{:S(2)}) collective-permute-start(s32[1,128]{1,0:T(1,128)S(1)} %bitcast.62), channel_id=1, source_target_pairs={{0,4},{1,5},{2,6},{3,7},{4,8},{5,9},{6,10},{7,11},{8,12},{9,13},{1... | collective-permute-start | bytes 1544 | tf_op jit(solution)/shard_map/ppermute | solution.py:14
  30.0 16.8 %copy-start.6 = (bf16[256,512]{1,0:T(8,128)(2,1)S(1)}, bf16[256,512]{1,0:T(8,128)(2,1)}, u32[]{:S(2)}) copy-start(bf16[256,512]{1,0:T(8,128)(2,1)} %param.13) | copy-start | bytes 786436
  30.0 12.2 %copy-start.5 = (bf16[1,4096,128]{2,1,0:T(8,128)(2,1)}, bf16[1,4096,128]{2,1,0:T(8,128)(2,1)S(1)}, u32[]{:S(2)}) copy-start(bf16[1,4096,128]{2,1,0:T(8,128)(2,1)S(1)} %collective-permute-done.6) | copy-start | bytes 3145732
  31.7 408.4 %collective-permute-start.7 = (bf16[2,4096,128]{2,1,0:T(8,128)(2,1)}, bf16[2,4096,128]{2,1,0:T(8,128)(2,1)S(1)}, u32[]{:S(2)}, u32[]{:S(2)}) collective-permute-start(bf16[2,4096,128]{2,1,0:T(8,128)(2,1)} %pad_maximum_fusion), channel_id=1, source_target_pairs={{0,2},{1,3},{2,4},{3,5},{4,6},{5,7},{6,8},{7,9},{8,10},{9,11},{10,... | collective-permute-start | bytes 6291464 | tf_op jit(solution)/shard_map/ppermute | solution.py:14
  42.4 384.8 %collective-permute-start.4 = (s32[2,128]{1,0:T(2,128)S(1)}, s32[2,128]{1,0:T(2,128)S(1)}, u32[]{:S(2)}, u32[]{:S(2)}) collective-permute-start(s32[2,128]{1,0:T(2,128)S(1)} %pad_add_fusion.1), channel_id=1, source_target_pairs={{0,2},{1,3},{2,4},{3,5},{4,6},{5,7},{6,8},{7,9},{8,10},{9,11},{10,... | collective-permute-start | bytes 3080 | tf_op jit(solution)/shard_map/ppermute | solution.py:14
  382.4 44.9 %copy-start.1 = (bf16[128,4096]{0,1:T(8,128)(2,1)S(1)}, bf16[128,4096]{0,1:T(8,128)(2,1)}, u32[]{:S(2)}) copy-start(bf16[128,4096]{0,1:T(8,128)(2,1)} %copy-done) | copy-start | bytes 3145732
  427.3 23.7 %collective-permute-start.5 = (bf16[1,4096,128]{2,1,0:T(8,128)(2,1)S(1)}, bf16[1,4096,128]{2,1,0:T(8,128)(2,1)S(1)}, u32[]{:S(2)}, u32[]{:S(2)}) collective-permute-start(bf16[1,4096,128]{2,1,0:T(8,128)(2,1)S(1)} %bitcast.53), channel_id=1, source_target_pairs={{0,4},{1,5},{2,6},{3,7},{4,8},{5,9},{6,10},{7,11},{8,12},{9,13},{1... | collective-permute-start | bytes 3145736 | tf_op jit(solution)/shard_map/ppermute | solution.py:14
  451.0 1.0 copy-start.9
  469.1 2.0 copy-start.4
where the time goes:
time: 474 us; the launch traced here: 472 us
  local copies, waits for them, and re-layouts  391 us (82%)
  starting transfers between devices  34.2 us (7%)
  matrix products  26.3 us (6%)
  other arithmetic  11.1 us (2%)
  waiting for transfers between devices  9.5 us (2%)
    gather x2, local copies, waits for them, and re-layouts, body(): far_taps = jnp.take(padded_filter, far_lag, axis=1)  303 us
    gather x2, local copies, waits for them, and re-layouts, body(): jnp.take(padded_filter, jnp.clip(near_lag, 0, STRETCH - 1), axis=1)  77.7 us
    ppermute x8, starting transfers between devices, passed_along(): lax.ppermute(value, axis, [(source, source + steps) for source in range(f...  34.2 us
    dot_general x1, matrix products, tile_product(): jnp.einsum('gtp,gkip->gkit', far_taps, gathered, preferred_element_type=j...  17.1 us
    ppermute x8, waiting for transfers between devices, passed_along(): lax.ppermute(value, axis, [(source, source + steps) for source in range(f...  9.5 us
  transfers between devices with their start and end apart: 8, of which 1 were waited for; matrix products, arithmetic and copies ran while one was open for 84% of the time, Pallas kernels for 0%

commit v1 on v0

v1 whole, which is shorter than its diff:
```python
import functools

import jax
import jax.numpy as jnp
from jax import lax
from jax.experimental import pallas as pl
from jax.experimental.pallas import tpu as pltpu
from jax.sharding import PartitionSpec as P

MAXDOC = 512
REACH = 4
RIM = 16
LANES = 128
CHUNKS = 8
MESH = pl.DeviceIdType.MESH


def kernel(
    count, gs_ref, k_ref, v_ref, gl_ref, doc_ref, se_ref, h_ref, out_ref,
    own, own_doc, rim_out, rim_in, got, got_doc, taps, rev, near_w, acc, agree, far_mask, near_mask,
    send_sem, recv_sem, doc_send, doc_recv, rim_send, rim_recv,
):
    rows, chans = gs_ref.shape
    tap_count = se_ref.shape[0]
    filters = h_ref.shape[0]
    width = chans // CHUNKS
    tiles = width // LANES
    fgroup = chans // filters
    per_tile = LANES // fgroup
    half = rows // 2
    span = MAXDOC + rows
    f32, bf16 = jnp.float32, jnp.bfloat16

    me = lax.axis_index("ctx")
    at = lax.rem(me, REACH)
    core = lax.rem(me, 2)
    upper = at // 2
    core_mate = me + 1 - 2 * core
    row_mate = me + 2 - 4 * upper
    has_prev = me >= REACH
    has_next = me + REACH < count
    is_first = me == 0
    is_last = me == count - 1

    barrier = pltpu.get_barrier_semaphore()

    def greet(target):
        pl.semaphore_signal(barrier, inc=1, device_id={"ctx": target}, device_id_type=MESH)

    greet(core_mate)
    greet(row_mate)
    pl.when(has_prev)(lambda: greet(me - REACH))
    pl.when(has_next)(lambda: greet(me + REACH))
    pl.when(me > 0)(lambda: greet(me - 1))
    pl.when(me < count - 1)(lambda: greet(me + 1))

    doc_row = jnp.broadcast_to(doc_ref[...].astype(f32), (rows, rows))
    doc_col = doc_row.T
    near_mask[...] = (doc_row == doc_col).astype(f32)
    own_doc[...] = doc_col.astype(bf16)
    kv_tail = k_ref[rows - RIM :, :].astype(f32) * v_ref[rows - RIM :, :].astype(f32)
    rim_out[:, :chans] = kv_tail.astype(bf16)
    rim_out[:, chans:] = doc_col[rows - RIM :, :].astype(bf16)

    peers = 2 + has_prev.astype(jnp.int32) + has_next.astype(jnp.int32)
    peers = peers + (me > 0).astype(jnp.int32) + (me < count - 1).astype(jnp.int32)
    pl.semaphore_wait(barrier, peers)

    def remote(src, dst, ssem, rsem, target):
        return pltpu.make_async_remote_copy(
            src_ref=src, dst_ref=dst, send_sem=ssem, recv_sem=rsem,
            device_id={"ctx": target}, device_id_type=MESH,
        )

    def rim_copy(target):
        return remote(rim_out, rim_in, rim_send, rim_recv, target)

    pl.when(me < count - 1)(lambda: rim_copy(me + 1).start())

    def block_copy(slot, j, src, target):
        return remote(src, got.at[slot, j], send_sem.at[slot, j], recv_sem.at[slot, j], target)

    def doc_copy(slot, src, target):
        return remote(src, got_doc.at[slot], doc_send.at[slot], doc_recv.at[slot], target)

    def start(slot, j, source, target):
        block, docs = (own.at[j], own_doc) if source is None else (got.at[source, j], got_doc.at[source])
        pl.when(j == 0)(lambda: doc_copy(slot, docs, target).start())
        block_copy(slot, j, block, target).start()

    def await_recv(slot, j):
        pl.when(j == 0)(lambda: doc_copy(slot, own_doc, core_mate).wait_recv())
        block_copy(slot, j, own.at[j], core_mate).wait_recv()

    def await_send(slot, j):
        pl.when(j == 0)(lambda: doc_copy(slot, own_doc, core_mate).wait_send())
        block_copy(slot, j, own.at[j], core_mate).wait_send()

    @pl.when(jnp.logical_not(has_prev))
    def _():
        got[0] = jnp.zeros(got.shape[1:], bf16)
        got_doc[0] = jnp.full(got_doc.shape[1:], -1.0, bf16)

    @pl.when(is_first)
    def _():
        rim_in[:, :chans] = jnp.zeros((RIM, chans), bf16)
        rim_in[:, chans:] = jnp.full((RIM, LANES), -1.0, bf16)

    for piece in range(span // LANES):
        lag = lax.broadcasted_iota(jnp.int32, (MAXDOC, LANES), 0)
        pos = lax.broadcasted_iota(jnp.int32, (MAXDOC, LANES), 1) + piece * LANES
        flip = jnp.where(lag + pos == MAXDOC, 1.0, 0.0).astype(bf16)
        rev[:, piece * LANES : (piece + 1) * LANES] = jnp.dot(
            h_ref[...], flip, preferred_element_type=f32
        )

    @pl.when(me > 0)
    def _():
        rim_copy(core_mate).wait_recv()

    doc_ext = jnp.concatenate([rim_in[:, chans:].astype(f32), doc_col], 0)
    for tap in range(tap_count):
        agree[tap] = (doc_ext[RIM - tap : RIM - tap + rows] == doc_col).astype(f32)

    def short_chunk(j, _):
        for tile in range(tiles):
            lanes = pl.ds(pl.multiple_of(j * width + tile * LANES, LANES), LANES)
            kv = (k_ref[:, lanes].astype(f32) * v_ref[:, lanes].astype(f32)).astype(bf16).astype(f32)
            ext = jnp.concatenate([rim_in[:, lanes].astype(f32), kv], 0)
            weights = se_ref[:, lanes]
            total = kv * weights[0:1, :]
            for tap in range(1, tap_count):
                shifted = ext[RIM - tap : RIM - tap + rows]
                total = total + (shifted * agree[tap]) * weights[tap : tap + 1, :]
            mixed = gs_ref[:, lanes].astype(f32) * total
            own[j, :, tile * LANES : (tile + 1) * LANES] = mixed.astype(bf16)
        pl.when(has_next)(lambda: start(0, j, None, me + REACH))
        pl.when(upper == 0)(lambda: start(2, j, None, row_mate))
        pl.when(core == 0)(lambda: start(1, j, None, core_mate))
        return 0

    lax.fori_loop(0, CHUNKS, short_chunk, 0)

    lane_group = lax.broadcasted_iota(jnp.int32, (1, LANES), 1) // fgroup

    def pick(result, height, lanes):
        picked = result[0:height, lanes]
        for g in range(1, per_tile):
            picked = jnp.where(lane_group == g, result[g * height : (g + 1) * height, lanes], picked)
        return picked

    def prepare(j, tile):
        ct = j * tiles + tile
        first = pl.multiple_of(ct * per_tile, per_tile)
        filt = rev[pl.ds(first, per_tile), :]
        for g in range(per_tile):
            line = filt[g : g + 1, :]
            low = pltpu.roll(jnp.broadcast_to(line, (half, span)), 0, 1, stride=1, stride_axis=0)
            tail = line[:, span - 2 * LANES :]
            high = pltpu.roll(jnp.broadcast_to(tail, (half, 2 * LANES)), half, 1, stride=1, stride_axis=0)
            base = pl.multiple_of((ct * per_tile + g) * half, half)
            taps[pl.ds(base, half), :] = low[:, :MAXDOC].astype(bf16)
            near_w[g * rows : g * rows + half, :] = (low[:, MAXDOC:] * near_mask[:half, :]).astype(bf16)
            near_w[g * rows + half : (g + 1) * rows, :] = (high[:, LANES:] * near_mask[half:, :]).astype(bf16)
        block = own[j, :, pl.ds(pl.multiple_of(tile * LANES, LANES), LANES)]
        result = jnp.dot(near_w[...], block, preferred_element_type=f32)
        acc[ct] = pick(result, rows, slice(0, LANES))

    leader = jnp.broadcast_to(doc_row[0:1, 0:1], (rows, LANES))
    near_mask_out = (doc_col == leader).astype(f32)
    agree[0] = near_mask_out

    def far(j, tile):
        ct = j * tiles + tile
        lanes = pl.ds(pl.multiple_of(tile * LANES, LANES), LANES)
        pieces = []
        for w in range(REACH):
            q = lax.rem(at + w, REACH)
            slot = (q // 2 + at // 2) % 2 * 2 + (q + at) % 2
            pieces.append(got[slot, j, :, lanes] * far_mask[w])
        left = jnp.concatenate(pieces, 0)
        right = jnp.concatenate([left[half:], jnp.zeros((half, LANES), bf16)], 0)
        base = pl.multiple_of(ct * per_tile * half, per_tile * half)
        result = jnp.dot(
            taps[pl.ds(base, per_tile * half), :],
            jnp.concatenate([left, right], 1),
            preferred_element_type=f32,
        )
        both = jnp.concatenate(
            [pick(result, half, slice(0, LANES)), pick(result, half, slice(LANES, 2 * LANES))], 0
        )
        total = acc[ct] + both * agree[0]
        wide = pl.ds(pl.multiple_of(ct * LANES, LANES), LANES)
        out_ref[:, wide] = (gl_ref[:, wide].astype(f32) * total).astype(bf16)

    def step(s, _):
        @pl.when(s < CHUNKS)
        def _():
            lax.fori_loop(0, tiles, lambda tile, c: (prepare(s, tile), c)[1], 0)
            pl.when(has_prev)(lambda: await_recv(0, s))
            pl.when(upper == 1)(lambda: start(2, s, 0, row_mate))
            pl.when(core == 1)(lambda: start(1, s, 0, core_mate))

        @pl.when((s >= 1) & (s < CHUNKS + 1))
        def _():
            await_recv(2, s - 1)
            start(3, s - 1, 2, core_mate)

        @pl.when(s >= 2)
        def _():
            j = s - 2
            await_recv(1, j)
            await_recv(3, j)

            @pl.when(j == 0)
            def _():
                for w in range(REACH):
                    q = lax.rem(at + w, REACH)
                    slot = (q // 2 + at // 2) % 2 * 2 + (q + at) % 2
                    far_mask[w] = (got_doc[slot].astype(f32) == leader).astype(bf16)

            lax.fori_loop(0, tiles, lambda tile, c: (far(j, tile), c)[1], 0)

        return 0

    lax.fori_loop(0, CHUNKS + 2, step, 0)

    def drain(j, _):
        pl.when(has_next)(lambda: await_send(0, j))
        for slot in (1, 2, 3):
            await_send(slot, j)
        return 0

    lax.fori_loop(0, CHUNKS, drain, 0)
    pl.when(me < count - 1)(lambda: rim_copy(core_mate).wait_send())


def body(gate_short, key_short, value_short, gate_long, doc_ids, se_filter, long_filter):
    rows, chans = gate_short.shape
    tap_count, filters = se_filter.shape
    fgroup = chans // filters
    count = lax.axis_size("ctx")
    assert rows * REACH == MAXDOC and rows == LANES and count % REACH == 0
    width = chans // CHUNKS
    bf16, f32 = jnp.bfloat16, jnp.float32
    widened = jnp.repeat(se_filter, fgroup, axis=1)
    vmem = pl.BlockSpec(memory_space=pltpu.VMEM)
    return pl.pallas_call(
        functools.partial(kernel, count),
        out_shape=jax.ShapeDtypeStruct((rows, chans), bf16),
        in_specs=[vmem] * 7,
        out_specs=vmem,
        scratch_shapes=[
            pltpu.VMEM((CHUNKS, rows, width), bf16),
            pltpu.VMEM((rows, LANES), bf16),
            pltpu.VMEM((RIM, chans + LANES), bf16),
            pltpu.VMEM((RIM, chans + LANES), bf16),
            pltpu.VMEM((REACH, CHUNKS, rows, width), bf16),
            pltpu.VMEM((REACH, rows, LANES), bf16),
            pltpu.VMEM((filters * rows // 2, MAXDOC), bf16),
            pltpu.VMEM((filters, MAXDOC + rows), f32),
            pltpu.VMEM((LANES // fgroup * rows, rows), bf16),
            pltpu.VMEM((chans // LANES, rows, LANES), f32),
            pltpu.VMEM((tap_count, rows, LANES), f32),
            pltpu.VMEM((REACH, rows, LANES), bf16),
            pltpu.VMEM((rows, rows), f32),
            pltpu.SemaphoreType.DMA((REACH, CHUNKS)),
            pltpu.SemaphoreType.DMA((REACH, CHUNKS)),
            pltpu.SemaphoreType.DMA((REACH,)),
            pltpu.SemaphoreType.DMA((REACH,)),
            pltpu.SemaphoreType.DMA,
            pltpu.SemaphoreType.DMA,
        ],
        compiler_params=pltpu.CompilerParams(
            collective_id=0, has_side_effects=True, vmem_limit_bytes=56 * 1024 * 1024
        ),
    )(gate_short, key_short, value_short, gate_long, doc_ids.reshape(1, rows), widened, long_filter)


def solution(mesh):
    placed = P(("groups", "ctx"), None)
    return jax.shard_map(
        body,
        mesh=mesh,
        in_specs=(placed, placed, placed, placed, P(("groups", "ctx")), P(), P()),
        out_specs=placed,
        check_vma=False,
    )
```

time: 474 us -> 54 us (0.11)
  local copies, waits for them, and re-layouts: 391 us -> 4.42 us
  Pallas kernels: 0 us -> 49.4 us
  starting transfers between devices: 34.2 us -> 0 us
  matrix products: 26.3 us -> 0 us
  other arithmetic: 11.1 us -> 0 us
  waiting for transfers between devices: 9.5 us -> 0 us
    gather x4 -> x0, local copies, waits for them, and re-layouts: 380 us -> none  [the longest x2 303 us: body(): far_taps = jnp.take(padded_filter, far_lag, axis=1)]
    pallas_call x0 -> x1, Pallas kernels: none -> 49.4 us  [body(): pl.pallas_call(functools.partial(kernel, count), out_shape=jax.ShapeDtype...]
    ppermute x8 -> x0, starting transfers between devices: 34.2 us -> none  [passed_along(): lax.ppermute(value, axis, [(source, source + steps) for source in range(f...]
    dot_general x2 -> x0, matrix products: 26.3 us -> none  [the longest x1 17.1 us: tile_product(): jnp.einsum('gtp,gkip->gkit', far_taps, gathered, preferred_element_type=j...]
    ppermute x8 -> x0, waiting for transfers between devices: 9.5 us -> none  [passed_along(): lax.ppermute(value, axis, [(source, source + steps) for source in range(f...]
    convert_element_type x4 -> x0, other arithmetic: 9.12 us -> none  [the longest x1 7.56 us: body(): mixed = (gate_short.astype(jnp.float32) * short_mix).astype(jnp.bfloat16)]
  transfers between devices with their start and end apart: 8 -> 0, of which waited for: 1 -> 0; matrix products, arithmetic and copies ran while one was open for 84% -> 0% of each run, Pallas kernels for 0% -> 0%
where the time goes in v1:
time: 54 us; the launch traced here: 53.8 us
  Pallas kernels  49.4 us (91%)
  local copies, waits for them, and re-layouts  4.42 us (8%)
    pallas_call x1, Pallas kernels, body(): pl.pallas_call(functools.partial(kernel, count), out_shape=jax.ShapeDtype...  49.4 us
    unnamed x1, local copies, waits for them, and re-layouts  2.29 us
    reshape x1, local copies, waits for them, and re-layouts, body(): widened = jnp.repeat(se_filter, fgroup, axis=1)  1.14 us

profile of v1, /device:TPU:0, one launch (start us, length us, event | category | flops | bytes accessed | tf_op | source)
XLA Modules:
  0.0 53.8 jit_solution(12663505778651287053)
XLA Ops:
  0.0 1.0 %broadcast_in_dim.3 = f32[7,256,16]{2,1,0:T(8,128)S(1)} broadcast(f32[7,256]{1,0:T(8,128)} %param.12), dimensions={0,1} | broadcast | bytes 121856 | tf_op jit(solution)/shard_map/broadcast_in_dim | solution.py:246
  1.0 1.1 %reshape.7.se_ref = f32[7,4096]{1,0:T(8,128)} reshape(f32[7,256,16]{2,1,0:T(8,128)S(1)} %broadcast_in_dim.3) | data formatting | bytes 229376 | tf_op jit(solution)/shard_map/reshape | solution.py:246
  2.1 49.4 %shard_map.73 = bf16[128,4096]{1,0:T(8,128)(2,1)} custom-call(bf16[128,4096]{1,0:T(8,128)(2,1)} %gs_ref.1, bf16[128,4096]{1,0:T(8,128)(2,1)} %k_ref.1, bf16[128,4096]{1,0:T(8,128)(2,1)} %v_ref.1, bf16[128,4096]{1,0:T(8,128)(2,1)} %gl_ref.1, s32[1,128]{1,0:T(1,128)} %bitcast.1, f32[7,4096]{1,0:T(8,128)} %reshape.7.se_ref, bf16[256,512]{1,0:T(8,128)(2,1)} %h_ref.1), custom_call_target="tpu_custom_call" | custom-call | tf_op jit(solution)/shard_map/pallas_call | solution.py:248
  51.5 2.3 %copy.9 = bf16[128,4096]{1,0:T(8,128)(2,1)} copy(bf16[128,4096]{1,0:T(8,128)(2,1)} %shard_map.73) | data formatting | bytes 2097152

commit v2 on v1

--- a/solution.py
+++ b/solution.py
@@ -10,8 +10,9 @@
 MAXDOC = 512
 REACH = 4
 RIM = 16
+STEP = 16
 LANES = 128
-CHUNKS = 8
+CHUNKS = 16
 MESH = pl.DeviceIdType.MESH
 
 
@@ -56,7 +57,7 @@
 
     doc_row = jnp.broadcast_to(doc_ref[...].astype(f32), (rows, rows))
     doc_col = doc_row.T
-    near_mask[...] = (doc_row == doc_col).astype(f32)
+    near_mask[...] = (doc_row == doc_col).astype(bf16)
     own_doc[...] = doc_col.astype(bf16)
     kv_tail = k_ref[rows - RIM :, :].astype(f32) * v_ref[rows - RIM :, :].astype(f32)
     rim_out[:, :chans] = kv_tail.astype(bf16)
@@ -96,24 +97,11 @@
         pl.when(j == 0)(lambda: doc_copy(slot, own_doc, core_mate).wait_send())
         block_copy(slot, j, own.at[j], core_mate).wait_send()
 
-    @pl.when(jnp.logical_not(has_prev))
-    def _():
-        got[0] = jnp.zeros(got.shape[1:], bf16)
-        got_doc[0] = jnp.full(got_doc.shape[1:], -1.0, bf16)
-
     @pl.when(is_first)
     def _():
         rim_in[:, :chans] = jnp.zeros((RIM, chans), bf16)
         rim_in[:, chans:] = jnp.full((RIM, LANES), -1.0, bf16)
 
-    for piece in range(span // LANES):
-        lag = lax.broadcasted_iota(jnp.int32, (MAXDOC, LANES), 0)
-        pos = lax.broadcasted_iota(jnp.int32, (MAXDOC, LANES), 1) + piece * LANES
-        flip = jnp.where(lag + pos == MAXDOC, 1.0, 0.0).astype(bf16)
-        rev[:, piece * LANES : (piece + 1) * LANES] = jnp.dot(
-            h_ref[...], flip, preferred_element_type=f32
-        )
-
     @pl.when(me > 0)
     def _():
         rim_copy(core_mate).wait_recv()
@@ -123,11 +111,17 @@
         agree[tap] = (doc_ext[RIM - tap : RIM - tap + rows] == doc_col).astype(f32)
 
     def short_chunk(j, _):
+        source = lax.broadcasted_iota(jnp.int32, (filters, width), 0)
+        target = lax.broadcasted_iota(jnp.int32, (filters, width), 1) // fgroup
+        spread = (source - j * (width // fgroup) == target).astype(f32)
+        widened = jnp.dot(
+            se_ref[...], spread, precision=lax.Precision.HIGHEST, preferred_element_type=f32
+        )
         for tile in range(tiles):
             lanes = pl.ds(pl.multiple_of(j * width + tile * LANES, LANES), LANES)
             kv = (k_ref[:, lanes].astype(f32) * v_ref[:, lanes].astype(f32)).astype(bf16).astype(f32)
             ext = jnp.concatenate([rim_in[:, lanes].astype(f32), kv], 0)
-            weights = se_ref[:, lanes]
+            weights = widened[:, tile * LANES : (tile + 1) * LANES]
             total = kv * weights[0:1, :]
             for tap in range(1, tap_count):
                 shifted = ext[RIM - tap : RIM - tap + rows]
@@ -141,6 +135,19 @@
 
     lax.fori_loop(0, CHUNKS, short_chunk, 0)
 
+    @pl.when(jnp.logical_not(has_prev))
+    def _():
+        got[0] = jnp.zeros(got.shape[1:], bf16)
+        got_doc[0] = jnp.full(got_doc.shape[1:], -1.0, bf16)
+
+    for piece in range(span // LANES):
+        lag = lax.broadcasted_iota(jnp.int32, (MAXDOC, LANES), 0)
+        pos = lax.broadcasted_iota(jnp.int32, (MAXDOC, LANES), 1) + piece * LANES
+        flip = jnp.where(lag + pos == MAXDOC, 1.0, 0.0).astype(bf16)
+        rev[:, piece * LANES : (piece + 1) * LANES] = jnp.dot(
+            h_ref[...], flip, preferred_element_type=f32
+        )
+
     lane_group = lax.broadcasted_iota(jnp.int32, (1, LANES), 1) // fgroup
 
     def pick(result, height, lanes):
@@ -154,14 +161,19 @@
         first = pl.multiple_of(ct * per_tile, per_tile)
         filt = rev[pl.ds(first, per_tile), :]
         for g in range(per_tile):
-            line = filt[g : g + 1, :]
-            low = pltpu.roll(jnp.broadcast_to(line, (half, span)), 0, 1, stride=1, stride_axis=0)
-            tail = line[:, span - 2 * LANES :]
-            high = pltpu.roll(jnp.broadcast_to(tail, (half, 2 * LANES)), half, 1, stride=1, stride_axis=0)
-            base = pl.multiple_of((ct * per_tile + g) * half, half)
-            taps[pl.ds(base, half), :] = low[:, :MAXDOC].astype(bf16)
-            near_w[g * rows : g * rows + half, :] = (low[:, MAXDOC:] * near_mask[:half, :]).astype(bf16)
-            near_w[g * rows + half : (g + 1) * rows, :] = (high[:, LANES:] * near_mask[half:, :]).astype(bf16)
+            line = jnp.broadcast_to(filt[g : g + 1, :], (STEP, span))
+            base = pltpu.roll(line, 0, 1, stride=1, stride_axis=0).astype(bf16)
+            tail = base[:, span - 2 * LANES :]
+            for r in range(rows // STEP):
+                low = slice(r * STEP, (r + 1) * STEP)
+                if r * STEP < half:
+                    turned = base if r == 0 else pltpu.roll(base, r * STEP, 1)
+                    at_row = pl.multiple_of((ct * per_tile + g) * half + r * STEP, STEP)
+                    taps[pl.ds(at_row, STEP), :] = turned[:, :MAXDOC]
+                    near = turned[:, MAXDOC:]
+                else:
+                    near = pltpu.roll(tail, r * STEP, 1)[:, LANES:]
+                near_w[g * rows + r * STEP : g * rows + (r + 1) * STEP, :] = near * near_mask[low, :]
         block = own[j, :, pl.ds(pl.multiple_of(tile * LANES, LANES), LANES)]
         result = jnp.dot(near_w[...], block, preferred_element_type=f32)
         acc[ct] = pick(result, rows, slice(0, LANES))
@@ -243,7 +255,6 @@
     assert rows * REACH == MAXDOC and rows == LANES and count % REACH == 0
     width = chans // CHUNKS
     bf16, f32 = jnp.bfloat16, jnp.float32
-    widened = jnp.repeat(se_filter, fgroup, axis=1)
     vmem = pl.BlockSpec(memory_space=pltpu.VMEM)
     return pl.pallas_call(
         functools.partial(kernel, count),
@@ -263,7 +274,7 @@
             pltpu.VMEM((chans // LANES, rows, LANES), f32),
             pltpu.VMEM((tap_count, rows, LANES), f32),
             pltpu.VMEM((REACH, rows, LANES), bf16),
-            pltpu.VMEM((rows, rows), f32),
+            pltpu.VMEM((rows, rows), bf16),
             pltpu.SemaphoreType.DMA((REACH, CHUNKS)),
             pltpu.SemaphoreType.DMA((REACH, CHUNKS)),
             pltpu.SemaphoreType.DMA((REACH,)),
@@ -274,7 +285,7 @@
         compiler_params=pltpu.CompilerParams(
             collective_id=0, has_side_effects=True, vmem_limit_bytes=56 * 1024 * 1024
         ),
-    )(gate_short, key_short, value_short, gate_long, doc_ids.reshape(1, rows), widened, long_filter)
+    )(gate_short, key_short, value_short, gate_long, doc_ids.reshape(1, rows), se_filter, long_filter)
 
 
 def solution(mesh):

time: 54 us -> 54 us (level)
  local copies, waits for them, and re-layouts: 4.42 us -> 2.29 us
  Pallas kernels: 49.4 us -> 51.5 us
    pallas_call x1, Pallas kernels: 49.4 us -> 51.5 us  [body(): pl.pallas_call(functools.partial(kernel, count), out_shape=jax.ShapeDtype...]
    reshape x1 -> x0, local copies, waits for them, and re-layouts: 1.14 us -> none  [body(): widened = jnp.repeat(se_filter, fgroup, axis=1)]
    broadcast_in_dim x1 -> x0, local copies, waits for them, and re-layouts: 0.99 us -> none  [body(): widened = jnp.repeat(se_filter, fgroup, axis=1)]
where the time goes in v2:
time: 54 us; the launch traced here: 53.8 us
  Pallas kernels  51.5 us (95%)
  local copies, waits for them, and re-layouts  2.29 us (4%)
    pallas_call x1, Pallas kernels, body(): pl.pallas_call(functools.partial(kernel, count), out_shape=jax.ShapeDtype...  51.5 us
    unnamed x1, local copies, waits for them, and re-layouts  2.29 us

profile of v2, /device:TPU:0, one launch (start us, length us, event | category | flops | bytes accessed | tf_op | source)
XLA Modules:
  0.0 53.8 jit_solution(5964937434375803004)
XLA Ops:
  0.0 51.5 %shard_map.73 = bf16[128,4096]{1,0:T(8,128)(2,1)} custom-call(bf16[128,4096]{1,0:T(8,128)(2,1)} %gs_ref.1, bf16[128,4096]{1,0:T(8,128)(2,1)} %k_ref.1, bf16[128,4096]{1,0:T(8,128)(2,1)} %v_ref.1, bf16[128,4096]{1,0:T(8,128)(2,1)} %gl_ref.1, s32[1,128]{1,0:T(1,128)} %bitcast.1, f32[7,256]{1,0:T(8,128)} %se_ref.1, bf16[256,512]{1,0:T(8,128)(2,1)} %h_ref.1), custom_call_target="tpu_custom_call" | custom-call | tf_op jit(solution)/shard_map/pallas_call | solution.py:259
  51.5 2.3 %copy.9 = bf16[128,4096]{1,0:T(8,128)(2,1)} copy(bf16[128,4096]{1,0:T(8,128)(2,1)} %shard_map.73) | data formatting | bytes 2097152

commit v3 on v2

--- a/solution.py
+++ b/solution.py
@@ -29,6 +29,7 @@
     fgroup = chans // filters
     per_tile = LANES // fgroup
     half = rows // 2
+    packed = per_tile // 2
     span = MAXDOC + rows
     f32, bf16 = jnp.float32, jnp.bfloat16
 
@@ -110,13 +111,19 @@
     for tap in range(tap_count):
         agree[tap] = (doc_ext[RIM - tap : RIM - tap + rows] == doc_col).astype(f32)
 
+    left_over, terms = se_ref[...], []
+    for _ in range(3):
+        term = left_over.astype(bf16).astype(f32)
+        left_over = left_over - term
+        terms += [term, jnp.zeros((8 - tap_count, filters), f32)]
+    se_parts = jnp.concatenate(terms, 0).astype(bf16)
+
     def short_chunk(j, _):
         source = lax.broadcasted_iota(jnp.int32, (filters, width), 0)
         target = lax.broadcasted_iota(jnp.int32, (filters, width), 1) // fgroup
-        spread = (source - j * (width // fgroup) == target).astype(f32)
-        widened = jnp.dot(
-            se_ref[...], spread, precision=lax.Precision.HIGHEST, preferred_element_type=f32
-        )
+        spread = jnp.where(source - j * (width // fgroup) == target, 1.0, 0.0).astype(bf16)
+        parts = jnp.dot(se_parts, spread, preferred_element_type=f32)
+        widened = parts[0:tap_count] + parts[8 : 8 + tap_count] + parts[16 : 16 + tap_count]
         for tile in range(tiles):
             lanes = pl.ds(pl.multiple_of(j * width + tile * LANES, LANES), LANES)
             kv = (k_ref[:, lanes].astype(f32) * v_ref[:, lanes].astype(f32)).astype(bf16).astype(f32)
@@ -173,10 +180,19 @@
                     near = turned[:, MAXDOC:]
                 else:
                     near = pltpu.roll(tail, r * STEP, 1)[:, LANES:]
-                near_w[g * rows + r * STEP : g * rows + (r + 1) * STEP, :] = near * near_mask[low, :]
-        block = own[j, :, pl.ds(pl.multiple_of(tile * LANES, LANES), LANES)]
-        result = jnp.dot(near_w[...], block, preferred_element_type=f32)
-        acc[ct] = pick(result, rows, slice(0, LANES))
+                e, side = g % packed, g // packed
+                near_w[tile, e * rows + r * STEP : e * rows + (r + 1) * STEP, side * rows : (side + 1) * rows] = (
+                    near * near_mask[low, :]
+                )
+        block = own[j, :, tile * LANES : (tile + 1) * LANES]
+        none = jnp.zeros_like(block)
+        first_side = lax.broadcasted_iota(jnp.int32, (rows, LANES), 1) < LANES // 2
+        block = jnp.concatenate([jnp.where(first_side, block, none), jnp.where(first_side, none, block)], 0)
+        result = jnp.dot(near_w[tile], block, preferred_element_type=f32)
+        picked = result[0:rows]
+        for e in range(1, packed):
+            picked = jnp.where(lane_group % packed == e, result[e * rows : (e + 1) * rows], picked)
+        acc[ct] = picked
 
     leader = jnp.broadcast_to(doc_row[0:1, 0:1], (rows, LANES))
     near_mask_out = (doc_col == leader).astype(f32)
@@ -184,7 +200,7 @@
 
     def far(j, tile):
         ct = j * tiles + tile
-        lanes = pl.ds(pl.multiple_of(tile * LANES, LANES), LANES)
+        lanes = slice(tile * LANES, (tile + 1) * LANES)
         pieces = []
         for w in range(REACH):
             q = lax.rem(at + w, REACH)
@@ -208,7 +224,8 @@
     def step(s, _):
         @pl.when(s < CHUNKS)
         def _():
-            lax.fori_loop(0, tiles, lambda tile, c: (prepare(s, tile), c)[1], 0)
+            for tile in range(tiles):
+                prepare(s, tile)
             pl.when(has_prev)(lambda: await_recv(0, s))
             pl.when(upper == 1)(lambda: start(2, s, 0, row_mate))
             pl.when(core == 1)(lambda: start(1, s, 0, core_mate))
@@ -231,7 +248,8 @@
                     slot = (q // 2 + at // 2) % 2 * 2 + (q + at) % 2
                     far_mask[w] = (got_doc[slot].astype(f32) == leader).astype(bf16)
 
-            lax.fori_loop(0, tiles, lambda tile, c: (far(j, tile), c)[1], 0)
+            for tile in range(tiles):
+                far(j, tile)
 
         return 0
 
@@ -270,7 +288,7 @@
             pltpu.VMEM((REACH, rows, LANES), bf16),
             pltpu.VMEM((filters * rows // 2, MAXDOC), bf16),
             pltpu.VMEM((filters, MAXDOC + rows), f32),
-            pltpu.VMEM((LANES // fgroup * rows, rows), bf16),
+            pltpu.VMEM((width // LANES, LANES // fgroup // 2 * rows, 2 * rows), bf16),
             pltpu.VMEM((chans // LANES, rows, LANES), f32),
             pltpu.VMEM((tap_count, rows, LANES), f32),
             pltpu.VMEM((REACH, rows, LANES), bf16),

time: 54 us -> 52.8 us (0.978)
  Pallas kernels: 51.5 us -> 50.4 us
    pallas_call x1, Pallas kernels: 51.5 us -> 50.4 us  [body(): pl.pallas_call(functools.partial(kernel, count), out_shape=jax.ShapeDtype...]
where the time goes in v3:
time: 52.8 us; the launch traced here: 52.7 us
  Pallas kernels  50.4 us (95%)
  local copies, waits for them, and re-layouts  2.29 us (4%)
    pallas_call x1, Pallas kernels, body(): pl.pallas_call(functools.partial(kernel, count), out_shape=jax.ShapeDtype...  50.4 us
    unnamed x1, local copies, waits for them, and re-layouts  2.29 us

profile of v3, /device:TPU:0, one launch (start us, length us, event | category | flops | bytes accessed | tf_op | source)
XLA Modules:
  0.0 52.7 jit_solution(11442885829504455579)
XLA Ops:
  0.0 50.4 %shard_map.73 = bf16[128,4096]{1,0:T(8,128)(2,1)} custom-call(bf16[128,4096]{1,0:T(8,128)(2,1)} %gs_ref.1, bf16[128,4096]{1,0:T(8,128)(2,1)} %k_ref.1, bf16[128,4096]{1,0:T(8,128)(2,1)} %v_ref.1, bf16[128,4096]{1,0:T(8,128)(2,1)} %gl_ref.1, s32[1,128]{1,0:T(1,128)} %bitcast.1, f32[7,256]{1,0:T(8,128)} %se_ref.1, bf16[256,512]{1,0:T(8,128)(2,1)} %h_ref.1), custom_call_target="tpu_custom_call" | custom-call | tf_op jit(solution)/shard_map/pallas_call | solution.py:277
  50.4 2.3 %copy.9 = bf16[128,4096]{1,0:T(8,128)(2,1)} copy(bf16[128,4096]{1,0:T(8,128)(2,1)} %shard_map.73) | data formatting | bytes 2097152

commit v4 on v2

--- a/solution.py
+++ b/solution.py
@@ -110,13 +110,19 @@
     for tap in range(tap_count):
         agree[tap] = (doc_ext[RIM - tap : RIM - tap + rows] == doc_col).astype(f32)
 
+    left_over, terms = se_ref[...], []
+    for _ in range(3):
+        term = left_over.astype(bf16).astype(f32)
+        left_over = left_over - term
+        terms += [term, jnp.zeros((8 - tap_count, filters), f32)]
+    se_parts = jnp.concatenate(terms, 0).astype(bf16)
+
     def short_chunk(j, _):
         source = lax.broadcasted_iota(jnp.int32, (filters, width), 0)
         target = lax.broadcasted_iota(jnp.int32, (filters, width), 1) // fgroup
-        spread = (source - j * (width // fgroup) == target).astype(f32)
-        widened = jnp.dot(
-            se_ref[...], spread, precision=lax.Precision.HIGHEST, preferred_element_type=f32
-        )
+        spread = jnp.where(source - j * (width // fgroup) == target, 1.0, 0.0).astype(bf16)
+        parts = jnp.dot(se_parts, spread, preferred_element_type=f32)
+        widened = parts[0:tap_count] + parts[8 : 8 + tap_count] + parts[16 : 16 + tap_count]
         for tile in range(tiles):
             lanes = pl.ds(pl.multiple_of(j * width + tile * LANES, LANES), LANES)
             kv = (k_ref[:, lanes].astype(f32) * v_ref[:, lanes].astype(f32)).astype(bf16).astype(f32)
@@ -184,7 +190,7 @@
 
     def far(j, tile):
         ct = j * tiles + tile
-        lanes = pl.ds(pl.multiple_of(tile * LANES, LANES), LANES)
+        lanes = slice(tile * LANES, (tile + 1) * LANES)
         pieces = []
         for w in range(REACH):
             q = lax.rem(at + w, REACH)
@@ -231,7 +237,8 @@
                     slot = (q // 2 + at // 2) % 2 * 2 + (q + at) % 2
                     far_mask[w] = (got_doc[slot].astype(f32) == leader).astype(bf16)
 
-            lax.fori_loop(0, tiles, lambda tile, c: (far(j, tile), c)[1], 0)
+            for tile in range(tiles):
+                far(j, tile)
 
         return 0
 

time: 54 us -> 49.5 us (0.917)
  Pallas kernels: 51.5 us -> 47 us
    pallas_call x1, Pallas kernels: 51.5 us -> 47 us  [body(): pl.pallas_call(functools.partial(kernel, count), out_shape=jax.ShapeDtype...]
where the time goes in v4:
time: 49.5 us; the launch traced here: 49.3 us
  Pallas kernels  47 us (95%)
  local copies, waits for them, and re-layouts  2.29 us (5%)
    pallas_call x1, Pallas kernels, body(): pl.pallas_call(functools.partial(kernel, count), out_shape=jax.ShapeDtype...  47 us
    unnamed x1, local copies, waits for them, and re-layouts  2.29 us

profile of v4, /device:TPU:0, one launch (start us, length us, event | category | flops | bytes accessed | tf_op | source)
XLA Modules:
  0.0 49.3 jit_solution(3681933452997103989)
XLA Ops:
  0.0 47.0 %shard_map.73 = bf16[128,4096]{1,0:T(8,128)(2,1)} custom-call(bf16[128,4096]{1,0:T(8,128)(2,1)} %gs_ref.1, bf16[128,4096]{1,0:T(8,128)(2,1)} %k_ref.1, bf16[128,4096]{1,0:T(8,128)(2,1)} %v_ref.1, bf16[128,4096]{1,0:T(8,128)(2,1)} %gl_ref.1, s32[1,128]{1,0:T(1,128)} %bitcast.1, f32[7,256]{1,0:T(8,128)} %se_ref.1, bf16[256,512]{1,0:T(8,128)(2,1)} %h_ref.1), custom_call_target="tpu_custom_call" | custom-call | tf_op jit(solution)/shard_map/pallas_call | solution.py:266
  47.0 2.3 %copy.9 = bf16[128,4096]{1,0:T(8,128)(2,1)} copy(bf16[128,4096]{1,0:T(8,128)(2,1)} %shard_map.73) | data formatting | bytes 2097152

commit v5 on v4

--- a/solution.py
+++ b/solution.py
@@ -11,6 +11,7 @@
 REACH = 4
 RIM = 16
 STEP = 16
+LAG = 2
 LANES = 128
 CHUNKS = 16
 MESH = pl.DeviceIdType.MESH
@@ -219,14 +220,14 @@
             pl.when(upper == 1)(lambda: start(2, s, 0, row_mate))
             pl.when(core == 1)(lambda: start(1, s, 0, core_mate))
 
-        @pl.when((s >= 1) & (s < CHUNKS + 1))
+        @pl.when((s >= LAG) & (s < CHUNKS + LAG))
         def _():
-            await_recv(2, s - 1)
-            start(3, s - 1, 2, core_mate)
-
-        @pl.when(s >= 2)
+            await_recv(2, s - LAG)
+            start(3, s - LAG, 2, core_mate)
+
+        @pl.when(s >= 2 * LAG)
         def _():
-            j = s - 2
+            j = s - 2 * LAG
             await_recv(1, j)
             await_recv(3, j)
 
@@ -242,7 +243,7 @@
 
         return 0
 
-    lax.fori_loop(0, CHUNKS + 2, step, 0)
+    lax.fori_loop(0, CHUNKS + 2 * LAG, step, 0)
 
     def drain(j, _):
         pl.when(has_next)(lambda: await_send(0, j))

time: 49.5 us -> 48.9 us (0.988)
  Pallas kernels: 47 us -> 46.5 us
    pallas_call x1, Pallas kernels: 47 us -> 46.5 us  [body(): pl.pallas_call(functools.partial(kernel, count), out_shape=jax.ShapeDtype...]
where the time goes in v5:
time: 48.9 us; the launch traced here: 48.8 us
  Pallas kernels  46.5 us (95%)
  local copies, waits for them, and re-layouts  2.29 us (5%)
    pallas_call x1, Pallas kernels, body(): pl.pallas_call(functools.partial(kernel, count), out_shape=jax.ShapeDtype...  46.5 us
    unnamed x1, local copies, waits for them, and re-layouts  2.29 us

profile of v5, /device:TPU:0, one launch (start us, length us, event | category | flops | bytes accessed | tf_op | source)
XLA Modules:
  0.0 48.8 jit_solution(10199544414141699044)
XLA Ops:
  0.0 46.5 %shard_map.73 = bf16[128,4096]{1,0:T(8,128)(2,1)} custom-call(bf16[128,4096]{1,0:T(8,128)(2,1)} %gs_ref.1, bf16[128,4096]{1,0:T(8,128)(2,1)} %k_ref.1, bf16[128,4096]{1,0:T(8,128)(2,1)} %v_ref.1, bf16[128,4096]{1,0:T(8,128)(2,1)} %gl_ref.1, s32[1,128]{1,0:T(1,128)} %bitcast.1, f32[7,256]{1,0:T(8,128)} %se_ref.1, bf16[256,512]{1,0:T(8,128)(2,1)} %h_ref.1), custom_call_target="tpu_custom_call" | custom-call | tf_op jit(solution)/shard_map/pallas_call | solution.py:267
  46.5 2.3 %copy.9 = bf16[128,4096]{1,0:T(8,128)(2,1)} copy(bf16[128,4096]{1,0:T(8,128)(2,1)} %shard_map.73) | data formatting | bytes 2097152

commit v6 on v5

--- a/solution.py
+++ b/solution.py
@@ -11,9 +11,9 @@
 REACH = 4
 RIM = 16
 STEP = 16
-LAG = 2
+LAG = 1
 LANES = 128
-CHUNKS = 16
+CHUNKS = 8
 MESH = pl.DeviceIdType.MESH
 
 

time: 48.9 us -> 46.3 us (0.947)
  Pallas kernels: 46.5 us -> 43.9 us
    pallas_call x1, Pallas kernels: 46.5 us -> 43.9 us  [body(): pl.pallas_call(functools.partial(kernel, count), out_shape=jax.ShapeDtype...]
where the time goes in v6:
time: 46.3 us; the launch traced here: 46.2 us
  Pallas kernels  43.9 us (95%)
  local copies, waits for them, and re-layouts  2.29 us (5%)
    pallas_call x1, Pallas kernels, body(): pl.pallas_call(functools.partial(kernel, count), out_shape=jax.ShapeDtype...  43.9 us
    unnamed x1, local copies, waits for them, and re-layouts  2.29 us

profile of v6, /device:TPU:0, one launch (start us, length us, event | category | flops | bytes accessed | tf_op | source)
XLA Modules:
  0.0 46.2 jit_solution(5442845827704111965)
XLA Ops:
  0.0 43.9 %shard_map.73 = bf16[128,4096]{1,0:T(8,128)(2,1)} custom-call(bf16[128,4096]{1,0:T(8,128)(2,1)} %gs_ref.1, bf16[128,4096]{1,0:T(8,128)(2,1)} %k_ref.1, bf16[128,4096]{1,0:T(8,128)(2,1)} %v_ref.1, bf16[128,4096]{1,0:T(8,128)(2,1)} %gl_ref.1, s32[1,128]{1,0:T(1,128)} %bitcast.1, f32[7,256]{1,0:T(8,128)} %se_ref.1, bf16[256,512]{1,0:T(8,128)(2,1)} %h_ref.1), custom_call_target="tpu_custom_call" | custom-call | tf_op jit(solution)/shard_map/pallas_call | solution.py:267
  43.9 2.3 %copy.9 = bf16[128,4096]{1,0:T(8,128)(2,1)} copy(bf16[128,4096]{1,0:T(8,128)(2,1)} %shard_map.73) | data formatting | bytes 2097152
